TPU v7x, 32 devices: a whole 2x2x4 slice. The times are simulated.
32 devices in a mesh: grp: 2 (over y), brick: 16 (over z, x, core).
Axes of the slice: x: 2, y: 2, z: 4, core: 2. Of those that a mesh axis runs over, the one named last changes fastest.
Arguments:
- low_factor: float32 [64, 16, 32, 512], P('brick', None, None, 'grp'), may hold values from -70 to 70, as said below
- test_matrix: float32 [512, 256], P('grp'), may hold values from -0.25 to 0.25
Outputs:
- basis: float32 [64, 16, 32, 256], P('brick')
- projected: float32 [256, 512], P(None, 'grp')
Inputs may be any that keep to these rules, and one draw needn't show every extreme that they name: `low_factor`: A dense real factor.
All inputs are finite; a program needn't handle non-finite values.
Results may differ from a plain program's by a relative error of at most 0.0003.
Values sent between devices are 32-bit elements; how exact they have to be, the bound alone decides.
A program may use at most 64 MiB of HBM per device.

v0:
```python
import jax
import jax.numpy as jnp
from jax import lax
from jax.sharding import PartitionSpec as P

DIFF = 0.12
CONV = 0.08
HIGH = lax.Precision.HIGHEST


def with_halo(block, sides, width):
    for axis, dim in sides:
        count = lax.axis_size(axis)
        forward = [(i, i + 1) for i in range(count - 1)]
        backward = [(target, source) for source, target in forward]
        low = lax.ppermute(
            lax.slice_in_dim(block, block.shape[dim] - width, None, axis=dim), axis, forward
        )
        high = lax.ppermute(lax.slice_in_dim(block, 0, width, axis=dim), axis, backward)
        block = jnp.concatenate([low, block, high], axis=dim)
    return block


def local_apply(extended):
    inner = extended[1:-1]
    padded = jnp.pad(inner, ((0, 0), (1, 1), (1, 1), (0, 0)))
    xminus = extended[:-2]
    xplus = extended[2:]
    beside_all = xminus + xplus + padded[:, :-2, 1:-1] + padded[:, 2:, 1:-1]
    beside_all = beside_all + padded[:, 1:-1, :-2] + padded[:, 1:-1, 2:]
    return inner - DIFF * beside_all - CONV * (xminus - xplus)


def apply_layer(field):
    return local_apply(with_halo(field, (("brick", 0),), 1))


def inner_product(left, right):
    return lax.dot_general(left, right, (((0,), (0,)), ((), ())), precision=HIGH)


def shards(low_factor, test_matrix):
    first = apply_layer(low_factor)
    second = apply_layer(first)
    slab_x, span_y, span_z, group_cols = second.shape
    flat = second.reshape(slab_x * span_y * span_z, group_cols)
    cells = flat.shape[0] * lax.axis_size("brick")
    sketch = lax.psum(
        jnp.dot(flat, test_matrix, precision=HIGH, preferred_element_type=jnp.float32), "grp"
    )
    gram = lax.psum(inner_product(sketch, sketch), "brick")
    lower = jnp.linalg.cholesky(gram)
    orthonormal = lax.linalg.triangular_solve(
        lower, sketch, left_side=False, lower=True, transpose_a=True
    )
    projected = lax.psum(inner_product(orthonormal, flat), "brick")
    basis = (orthonormal * jnp.sqrt(jnp.float32(cells))).reshape(
        slab_x, span_y, span_z, orthonormal.shape[1]
    )
    return (basis, projected)


def solution(mesh):
    return jax.shard_map(
        shards,
        mesh=mesh,
        in_specs=(P("brick", None, None, "grp"), P("grp", None)),
        out_specs=(P("brick", None, None, None), P(None, "grp")),
        check_vma=False,
    )
```

profile of v0, /device:TPU:0, one launch (start us, length us, event | category | flops | bytes accessed | tf_op | source)
XLA Modules:
  0.0 379.3 jit_solution(2512214408184303391)
XLA Ops:
  7.2 1.5 fusion.29
  8.7 1.3 collective-permute-start.1
  10.0 3.1 collective-permute-start
  13.1 1.5 collective-permute-done
  14.6 1.9 fusion.6
  16.6 1.3 collective-permute-start.3
  17.9 14.3 %collective-permute-start.2 = (f32[1,16,32,256]{3,2,1,0:T(8,128)S(1)}, f32[1,16,32,256]{3,2,1,0:T(8,128)S(1)}, u32[]{:S(2)}, u32[]{:S(2)}) collective-permute-start(f32[1,16,32,256]{3,2,1,0:T(8,128)S(1)} %get-tuple-element.21), channel_id=1, source_target_pairs={{0,1},{1,2},{2,3},{3,4},{4,5},{5,6},{6,7},{7,8},{8,9},{9,10},{10,1... | collective-permute-start | bytes 1572872 | tf_op jit(solution)/shard_map/ppermute | solution.py:16
  32.2 1.5 collective-permute-done.2
  33.7 2.0 fusion.13
  35.7 1.3 copy-done.2
  37.0 3.1 fusion.30
  40.2 73.6 %all-reduce.7.cloned.1.call-done = f32[2048,256]{1,0:T(8,128)} async-done(((f32[2048,256]{1,0:T(8,128)}), f32[2048,256]{1,0:T(8,128)}) %all-reduce.7.cloned.1.call-update) | async-done | bytes 2097168 | tf_op jit(solution)/shard_map/psum | solution.py:48
  113.9 6.4 %fusion.31 = f32[256,256]{0,1:T(8,128)} fusion(f32[2048,256]{1,0:T(8,128)} %all-reduce.7.cloned.1.call-done), kind=kOutput, calls=%fused_computation.63 | convolution fusion | flops 1610612736 | bytes 2359296 | tf_op jit(solution)/shard_map/dot_general | solution.py:39
  120.5 89.6 %all-reduce.9.cloned.1.call-done = f32[256,256]{0,1:T(8,128)} async-done(((f32[256,256]{0,1:T(8,128)}), f32[256,256]{0,1:T(8,128)}) %all-reduce.9.cloned.1.call-update) | async-done | bytes 262160 | tf_op jit(solution)/shard_map/psum | solution.py:51
  210.1 1.1 copy.5
  211.2 1.0 fusion.20
  212.2 11.7 %cholesky.50 = f32[128,128]{1,0:T(8,128)S(1)} custom-call(f32[128,128]{1,0:T(8,128)S(1)} %cholesky.118), custom_call_target="Cholesky" | custom-call | tf_op jit(solution)/shard_map/jit(cholesky)/cholesky | solution.py:52
  223.9 9.8 %custom-call.14 = f32[1,128,128]{1,2,0:T(8,128)S(1)} custom-call(f32[1,128,128]{2,1,0:T(8,128)S(1)} %get-tuple-element.27), custom_call_target="InvertDiagBlocksLowerTriangular" | custom-call | tf_op jit(solution)/shard_map/jit(cholesky)/cholesky | solution.py:52
  234.3 11.7 %cholesky.105 = f32[128,128]{1,0:T(8,128)S(1)} custom-call(f32[128,128]{1,0:T(8,128)S(1)} %convolution_subtract_fusion.1), custom_call_target="Cholesky" | custom-call | tf_op jit(solution)/shard_map/jit(cholesky)/cholesky | solution.py:52
  246.0 0.7 compare_reduce_fusion
  248.1 4.1 %while.1 = (s32[]{:T(128)}, f32[256,256]{1,0:T(8,128)S(1)}, s32[2,2]{1,0:T(2,128)S(1)}, f32[2,128,128]{2,1,0:T(8,128)S(1)}, s32[]{:T(128)}) while((s32[]{:T(128)}, f32[256,256]{1,0:T(8,128)S(1)}, s32[2,2]{1,0:T(2,128)S(1)}, f32[2,128,128]{2,1,0:T(8,128)S(1)}, s32[]{:T(128)}) %tuple.29), condition=%wide.while_cond, body=%wide.while_body.sunk | while | flops 2 | bytes 131189 | solution.py:53
  248.8 1.4 bitcast_dynamic-update-slice_fusion.2
  250.8 1.4 bitcast_dynamic-update-slice_fusion.2
  252.2 0.7 copy-done.5
  252.9 19.7 %custom-call.15 = f32[2,128,128]{1,2,0:T(8,128)S(1)} custom-call(f32[2,128,128]{2,1,0:T(8,128)S(1)} %get-tuple-element.9), custom_call_target="InvertDiagBlocksLowerTriangular" | custom-call | tf_op jit(solution)/shard_map/triangular_solve | solution.py:53
  272.5 1.0 fusion.18
  273.5 2.0 convolution_subtract_fusion
  275.5 1.0 fusion.21
  276.5 4.2 %fusion.14 = f32[256,256]{1,0:T(8,128)} fusion(f32[2048,256]{1,0:T(8,128)S(1)} %bitcast.40, f32[2048,128]{1,0:T(8,128)S(1)} %fusion.21, f32[2048,128]{1,0:T(8,128)S(1)} %fusion.18), kind=kOutput, calls=%fused_computation.30 | convolution fusion | flops 1611137024 | bytes 4456448 | tf_op jit(solution)/shard_map/dot_general | solution.py:39
  280.7 1.6 maximum_multiply_fusion
  282.3 88.8 %all-reduce.11.cloned.1.call-done = f32[256,256]{1,0:T(8,128)} async-done(((f32[256,256]{1,0:T(8,128)}), f32[256,256]{1,0:T(8,128)}) %all-reduce.11.cloned.1.call-update) | async-done | bytes 262160 | tf_op jit(solution)/shard_map/psum | solution.py:56
  371.1 1.7 copy.21
  (33 shorter events, 2.3 us)
Async XLA Ops:
  7.2 29.9 %copy-start = (f32[256,256]{1,0:T(8,128)S(1)}, f32[256,256]{1,0:T(8,128)}, u32[]{:S(2)}) copy-start(f32[256,256]{1,0:T(8,128)} %param.3) | copy-start | bytes 786436
  7.2 7.4 %copy-start.4 = (f32[4,16,32,256]{3,2,1,0:T(8,128)S(1)}, f32[4,16,32,256]{3,2,1,0:T(8,128)}, u32[]{:S(2)}) copy-start(f32[4,16,32,256]{3,2,1,0:T(8,128)} %param.2) | copy-start | bytes 6291460
  7.2 106.7 %all-reduce.7.cloned.1.call-start = ((), (), s32[]{:S(2)}) async-start(), calls=%async_computation | async-start | bytes 4194304 | tf_op jit(solution)/shard_map/psum | solution.py:48
  8.7 4.4 %collective-permute-start.1 = (f32[1,16,32,256]{3,2,1,0:T(8,128)S(1)}, f32[1,16,32,256]{3,2,1,0:T(8,128)S(1)}, u32[]{:S(2)}, u32[]{:S(2)}) collective-permute-start(f32[1,16,32,256]{3,2,1,0:T(8,128)S(1)} %get-tuple-element.22), channel_id=1, source_target_pairs={{1,0},{2,1},{3,2},{4,3},{5,4},{6,5},{7,6},{8,7},{9,8},{10,9},{11,1... | collective-permute-start | bytes 1572872 | tf_op jit(solution)/shard_map/ppermute | solution.py:19
  10.0 4.6 %collective-permute-start = (f32[1,16,32,256]{3,2,1,0:T(8,128)S(1)}, f32[1,16,32,256]{3,2,1,0:T(8,128)S(1)}, u32[]{:S(2)}, u32[]{:S(2)}) collective-permute-start(f32[1,16,32,256]{3,2,1,0:T(8,128)S(1)} %get-tuple-element.23), channel_id=1, source_target_pairs={{0,1},{1,2},{2,3},{3,4},{4,5},{5,6},{6,7},{7,8},{8,9},{9,10},{10,1... | collective-permute-start | bytes 1572872 | tf_op jit(solution)/shard_map/ppermute | solution.py:16
  16.6 15.7 %collective-permute-start.3 = (f32[1,16,32,256]{3,2,1,0:T(8,128)S(1)}, f32[1,16,32,256]{3,2,1,0:T(8,128)S(1)}, u32[]{:S(2)}, u32[]{:S(2)}) collective-permute-start(f32[1,16,32,256]{3,2,1,0:T(8,128)S(1)} %get-tuple-element.20), channel_id=1, source_target_pairs={{1,0},{2,1},{3,2},{4,3},{5,4},{6,5},{7,6},{8,7},{9,8},{10,9},{11,1... | collective-permute-start | bytes 1572872 | tf_op jit(solution)/shard_map/ppermute | solution.py:19
  17.9 15.8 %collective-permute-start.2 = (f32[1,16,32,256]{3,2,1,0:T(8,128)S(1)}, f32[1,16,32,256]{3,2,1,0:T(8,128)S(1)}, u32[]{:S(2)}, u32[]{:S(2)}) collective-permute-start(f32[1,16,32,256]{3,2,1,0:T(8,128)S(1)} %get-tuple-element.21), channel_id=1, source_target_pairs={{0,1},{1,2},{2,3},{3,4},{4,5},{5,6},{6,7},{7,8},{8,9},{9,10},{10,1... | collective-permute-start | bytes 1572872 | tf_op jit(solution)/shard_map/ppermute | solution.py:16
  35.7 1.4 copy-start.2
  40.2 169.9 %all-reduce.9.cloned.1.call-start = ((), (), s32[]{:S(2)}) async-start(), calls=%async_computation.1 | async-start | bytes 524288 | tf_op jit(solution)/shard_map/psum | solution.py:51
  120.2 152.3 %copy-start.1 = (f32[2048,256]{1,0:T(8,128)S(1)}, f32[2048,256]{1,0:T(8,128)}, u32[]{:S(2)}) copy-start(f32[2048,256]{1,0:T(8,128)} %all-reduce.7.cloned.1.call-done) | copy-start | bytes 6291460
  120.3 250.9 %all-reduce.11.cloned.1.call-start = ((), (), s32[]{:S(2)}) async-start(), calls=%async_computation.2 | async-start | bytes 524288 | tf_op jit(solution)/shard_map/psum | solution.py:56
  252.2 0.7 copy-start.5
  273.5 3.0 copy-start.3
Sparse Core Ops, SparseCore 0:
  40.3 73.5 all-reduce.6
  120.4 89.6 all-reduce.8
  280.9 90.2 all-reduce.10
where the time goes:
time: 380 us; the launch traced here: 379 us
  waiting for transfers between devices  255 us (67%)
  other arithmetic  60.1 us (16%)
  starting transfers between devices  20.3 us (5%)
  matrix products  18.1 us (5%)
  between operations  15.3 us (4%)
  local copies, waits for them, and re-layouts  10.3 us (3%)
    psum x1, waiting for transfers between devices, shards(): gram = lax.psum(inner_product(sketch, sketch), 'brick')  89.6 us
    psum x1, waiting for transfers between devices, shards(): projected = lax.psum(inner_product(orthonormal, flat), 'brick')  88.8 us
    psum x1, waiting for transfers between devices, shards(): lax.psum(jnp.dot(flat, test_matrix, precision=HIGH, preferred_element_typ...  73.6 us
    another operation x6, other arithmetic, shards(): lower = jnp.linalg.cholesky(gram)  34 us
    another operation x3, other arithmetic, shards(): lax.linalg.triangular_solve(lower, sketch, left_side=False, lower=True, t...  19.7 us
    ppermute x2, starting transfers between devices, with_halo(): lax.ppermute(lax.slice_in_dim(block, block.shape[dim] - width, None, axis...  17.4 us
    dot_general x2, matrix products, inner_product(): lax.dot_general(left, right, (((0,), (0,)), ((), ())), precision=HIGH)  10.6 us
  transfers between devices with their start and end apart: 7, of which 5 were waited for; matrix products, arithmetic and copies ran while one was open for 0% of the time, Pallas kernels for 0%

commit v1 on v0

v1 whole, which is shorter than its diff:
```python
import functools

import jax
import jax.numpy as jnp
from jax import lax
from jax.experimental import pallas as pl
from jax.experimental.pallas import tpu as pltpu
from jax.sharding import PartitionSpec as P

DIFF = 0.12
CONV = 0.08
HIGH = lax.Precision.HIGHEST
MESH = pl.DeviceIdType.MESH
BLOCK = 32


def dot(left, right, dims):
    return lax.dot_general(
        left, right, (dims, ((), ())), precision=HIGH, preferred_element_type=jnp.float32
    )


def chunk_ends(span_y, slab_x, groups):
    count = 4
    size = span_y // count
    if span_y % count or size < 3 or (slab_x * size) % groups or (slab_x * 2) % groups:
        return [(span_y, span_y, span_y)]
    ends = []
    for k in range(count):
        end = size * (k + 1)
        ends.append((end, end - 1, end - 2) if k < count - 1 else (end, end, end))
    return ends


def kernel(
    dims, x_hbm, omega, basis, projected,
    ext, first, grown, part, sketch, group_rx, gram, gram_rx, full, proj, proj_rx, proj_full, both,
    local_sem, halo_send, halo_recv, part_send, part_recv, back_send, back_recv, reduce_sem, gather_sem,
):
    groups, bricks, slab, span_y, span_z, cells = dims
    rank = omega.shape[1]
    cols = omega.shape[0]
    devices = groups * bricks
    me_g = lax.axis_index("grp")
    me_b = lax.axis_index("brick")
    me = me_g * bricks + me_b
    owners = min(bricks, rank // 8)
    strip = rank // owners
    ends = chunk_ends(span_y, slab, groups)

    def device(g, b):
        return {"grp": g, "brick": b}

    barrier = pltpu.get_barrier_semaphore()

    def greet(d, carry):
        other = lax.rem(me + d, devices)
        g = other // bricks
        pl.semaphore_signal(
            barrier, inc=1, device_id=device(g, other - g * bricks), device_id_type=MESH
        )
        return carry

    lax.fori_loop(1, devices, greet, 0)
    mine = pltpu.make_async_copy(
        x_hbm, ext.at[pl.ds(2, slab), pl.ds(1, span_y)], local_sem
    )
    mine.start()
    layer = (span_z, cols)
    for y in (0, span_y + 1):
        ext[:, y] = jnp.zeros((slab + 4,) + layer, jnp.float32)
        first[:, y] = jnp.zeros((slab + 2,) + layer, jnp.float32)

    @pl.when(me_b == 0)
    def _():
        ext[0:2] = jnp.zeros((2, span_y + 2) + layer, jnp.float32)

    @pl.when(me_b == bricks - 1)
    def _():
        ext[slab + 2 :] = jnp.zeros((2, span_y + 2) + layer, jnp.float32)

    pl.semaphore_wait(barrier, devices - 1)

    def halo(k, up):
        start = 0 if k == 0 else ends[k - 1][0]
        rows = ends[k][0] - start
        side = 0 if up else 1
        return pltpu.make_async_remote_copy(
            src_ref=x_hbm.at[pl.ds(slab - 2 if up else 0, 2), pl.ds(start, rows)],
            dst_ref=ext.at[pl.ds(0 if up else slab + 2, 2), pl.ds(1 + start, rows)],
            send_sem=halo_send.at[side, k],
            recv_sem=halo_recv.at[side, k],
            device_id=device(me_g, me_b + 1 if up else me_b - 1),
            device_id_type=MESH,
        )

    for k in range(len(ends)):
        @pl.when(me_b < bricks - 1)
        def _():
            halo(k, True).start()

        @pl.when(me_b > 0)
        def _():
            halo(k, False).start()

    mine.wait()

    def operate(mid, low, high, before, after):
        z = lax.broadcasted_iota(jnp.int32, mid.shape, mid.ndim - 2)
        down = jnp.where(z == 0, 0.0, pltpu.roll(mid, 1, mid.ndim - 2))
        up = jnp.where(z == span_z - 1, 0.0, pltpu.roll(mid, span_z - 1, mid.ndim - 2))
        beside = low + high + before + after + down + up
        return mid - DIFF * beside - CONV * (low - high)

    gate_low = jnp.where(me_b == 0, 0.0, 1.0)
    gate_high = jnp.where(me_b == bricks - 1, 0.0, 1.0)

    def first_row(y, carry):
        for i in range(slab + 2):
            value = operate(
                ext[i + 1, y + 1], ext[i, y + 1], ext[i + 2, y + 1], ext[i + 1, y], ext[i + 1, y + 2]
            )
            if i == 0:
                value = value * gate_low
            if i == slab + 1:
                value = value * gate_high
            first[i, y + 1] = value
        return carry

    def second_row(y, carry):
        values = []
        for i in range(slab):
            value = operate(
                first[i + 1, y + 1], first[i, y + 1], first[i + 2, y + 1],
                first[i + 1, y], first[i + 1, y + 2],
            )
            grown[y * slab + i] = value
            values.append(value)
        rows = jnp.concatenate(values, axis=0)
        terms = dot(rows, omega[...], ((1,), (0,)))
        part[pl.ds(y * slab, slab)] = terms.reshape(slab, span_z, rank)
        return carry

    def piece(k):
        start = 0 if k == 0 else ends[k - 1][2]
        pairs = (ends[k][2] - start) * slab // groups
        return start * slab, pairs

    def part_copy(k, d):
        start, pairs = piece(k)
        other = lax.rem(me_g + d, groups)
        return pltpu.make_async_remote_copy(
            src_ref=part.at[pl.ds(start + other * pairs, pairs)],
            dst_ref=group_rx.at[d - 1, pl.ds(start // groups, pairs)],
            send_sem=part_send.at[k, d - 1],
            recv_sem=part_recv.at[k, d - 1],
            device_id=device(other, me_b),
            device_id_type=MESH,
        )

    def back_copy(k, d):
        start, pairs = piece(k)
        other = lax.rem(me_g + d, groups)
        here = sketch.at[pl.ds(start + me_g * pairs, pairs)]
        return pltpu.make_async_remote_copy(
            src_ref=here,
            dst_ref=here,
            send_sem=back_send.at[k, d - 1],
            recv_sem=back_recv.at[k, d - 1],
            device_id=device(other, me_b),
            device_id_type=MESH,
        )

    def own_rows(k):
        start, pairs = piece(k)
        for d in range(1, groups):
            part_copy(k, d).wait_recv()

        def body(i, carry):
            at = start + me_g * pairs + i
            total = part[at]
            for d in range(groups - 1):
                total = total + group_rx[d, start // groups + i]
            sketch[at] = total
            return carry

        lax.fori_loop(0, pairs, body, 0)
        value = sketch[pl.ds(start + me_g * pairs, pairs)].reshape(pairs * span_z, rank)
        term = dot(value, value, ((0,), (0,)))
        if k == 0:
            gram[...] = term
        else:
            gram[...] += term

    for k, (end, end_first, end_second) in enumerate(ends):
        @pl.when(me_b > 0)
        def _():
            halo(k, True).wait_recv()

        @pl.when(me_b < bricks - 1)
        def _():
            halo(k, False).wait_recv()

        begin_first, begin_second = (0, 0) if k == 0 else ends[k - 1][1:]
        lax.fori_loop(begin_first, end_first, first_row, 0)
        lax.fori_loop(begin_second, end_second, second_row, 0)
        for d in range(1, groups):
            part_copy(k, d).start()
        if k > 0:
            own_rows(k - 1)
    own_rows(len(ends) - 1)

    def strip_at(o):
        return pl.ds(pl.multiple_of(o * strip, 8), strip)

    def to_owner(source, sink, sem, d, count, slot):
        other = lax.rem(me + d, devices) if count == devices else lax.rem(me_b + d, bricks)
        g = other // bricks if count == devices else me_g
        o = other - g * bricks if count == devices else other
        return o, pltpu.make_async_remote_copy(
            src_ref=source.at[strip_at(o)],
            dst_ref=sink.at[slot],
            send_sem=reduce_sem.at[sem, 0],
            recv_sem=reduce_sem.at[sem, 1],
            device_id=device(g, o),
            device_id_type=MESH,
        )

    def guarded(o, action):
        if owners == bricks:
            action()
        else:
            pl.when(o < owners)(action)

    def scatter_start(source, sink, sem, count, slot):
        def body(d, carry):
            def send():
                to_owner(source, sink, sem, d, count, slot)[1].start()

            o = lax.rem(me + d, bricks) if count == devices else lax.rem(me_b + d, bricks)
            guarded(o, send)
            return carry

        lax.fori_loop(1, count, body, 0)

        def keep():
            sink[slot] = source[strip_at(me_b)]

        guarded(me_b, keep)

    def bytes_wait(ref, sem):
        pltpu.make_async_copy(ref, ref, sem).wait()

    def scatter_finish(source, sink, sem, count, result):
        def receive():
            bytes_wait(sink.at[pl.ds(0, count - 1)], reduce_sem.at[sem, 1])

            def add(i, total):
                return total + sink[i]

            result[strip_at(me_b)] = lax.fori_loop(1, count, add, sink[0])

        guarded(me_b, receive)
        copies = count // bricks * owners
        if owners == bricks:
            bytes_wait(sink.at[pl.ds(0, copies - 1)], reduce_sem.at[sem, 0])
        else:
            @pl.when(me_b < owners)
            def _():
                bytes_wait(sink.at[pl.ds(0, copies - 1)], reduce_sem.at[sem, 0])

            @pl.when(me_b >= owners)
            def _():
                bytes_wait(sink.at[pl.ds(0, copies)], reduce_sem.at[sem, 0])

    def gather_start(result, sem):
        def body(d, carry):
            here = result.at[strip_at(me_b)]
            pltpu.make_async_remote_copy(
                src_ref=here,
                dst_ref=here,
                send_sem=gather_sem.at[sem, 0],
                recv_sem=gather_sem.at[sem, 1],
                device_id=device(me_g, lax.rem(me_b + d, bricks)),
                device_id_type=MESH,
            ).start()
            return carry

        def send():
            lax.fori_loop(1, bricks, body, 0)

        guarded(me_b, send)

    def gather_finish(result, sem, sink):
        rows = strip * (owners - 1)
        if owners == bricks:
            bytes_wait(result.at[pl.ds(0, rows)], gather_sem.at[sem, 1])
            bytes_wait(result.at[pl.ds(0, rows)], gather_sem.at[sem, 0])
        else:
            @pl.when(me_b < owners)
            def _():
                bytes_wait(result.at[pl.ds(0, rows)], gather_sem.at[sem, 1])
                bytes_wait(sink.at[pl.ds(0, bricks - 1)], gather_sem.at[sem, 0])

            @pl.when(me_b >= owners)
            def _():
                bytes_wait(result.at[...], gather_sem.at[sem, 1])

    scatter_start(gram, gram_rx, 0, devices, me)
    for k in range(len(ends)):
        for d in range(1, groups):
            back_copy(k, d).start()
    scatter_finish(gram, gram_rx, 0, devices, full)
    gather_start(full, 0)
    gather_finish(full, 0, gram_rx)

    both[:, 0:rank] = full[...]
    row = lax.broadcasted_iota(jnp.int32, (rank, rank), 0)
    col = lax.broadcasted_iota(jnp.int32, (rank, rank), 1)
    both[:, rank:] = jnp.where(row == col, 1.0, 0.0)

    def project():
        for k in range(len(ends)):
            for d in range(1, groups):
                back_copy(k, d).wait_recv()
        proj[...] = jnp.zeros_like(proj)

        @pl.loop(0, span_y)
        def _(y):
            left = sketch[pl.ds(y * slab, slab)].reshape(slab * span_z, rank)
            right = grown[pl.ds(y * slab, slab)].reshape(slab * span_z, cols)
            proj[...] += dot(left, right, ((0,), (0,)))

        scatter_start(proj, proj_rx, 1, bricks, me_b)

    def project_gather():
        scatter_finish(proj, proj_rx, 1, bricks, proj_full)
        gather_start(proj_full, 1)

    blocks = rank // BLOCK
    for block in range(blocks):
        if block == blocks // 2:
            project()
        if block == blocks - 1:
            project_gather()
        at = block * BLOCK
        panel = both[at : at + BLOCK, :]
        row = lax.broadcasted_iota(jnp.int32, (BLOCK, 1), 0)
        for j in range(BLOCK):
            pivot = panel[j : j + 1, :]
            scaled = pivot * (1.0 / pivot[:, at + j : at + j + 1])
            factor = jnp.where(row > j, panel[:, at + j : at + j + 1], 0.0)
            panel = panel - factor * scaled
        lane = lax.broadcasted_iota(jnp.int32, panel.shape, 1)
        full_row = lax.broadcasted_iota(jnp.int32, panel.shape, 0)
        diagonal = jnp.sum(
            jnp.where(lane == full_row + at, panel, 0.0), axis=1, keepdims=True
        )
        panel = panel * lax.rsqrt(diagonal)
        both[at : at + BLOCK, :] = panel
        if block < blocks - 1:
            below = dot(panel[:, 0:rank], panel, ((0,), (0,)))
            both[at + BLOCK :, :] = both[at + BLOCK :, :] - below[at + BLOCK :, :]

    inverse = both[:, rank:]
    scaled_inverse = inverse.T * jnp.sqrt(jnp.float32(cells))
    both[:, 0:rank] = scaled_inverse

    @pl.loop(0, span_y)
    def _(y):
        left = sketch[pl.ds(y * slab, slab)].reshape(slab * span_z, rank)
        value = dot(left, both[:, 0:rank], ((1,), (0,)))
        basis[:, y] = value.reshape(slab, span_z, rank)

    gather_finish(proj_full, 1, proj_rx)
    projected[...] = dot(both[:, rank:], proj_full[...], ((1,), (0,)))

    for k in range(len(ends)):
        @pl.when(me_b < bricks - 1)
        def _():
            halo(k, True).wait_send()

        @pl.when(me_b > 0)
        def _():
            halo(k, False).wait_send()

        for d in range(1, groups):
            part_copy(k, d).wait_send()
            back_copy(k, d).wait_send()


def shards(groups, bricks, low_factor, test_matrix):
    slab, span_y, span_z, cols = low_factor.shape
    rank = test_matrix.shape[1]
    pairs = slab * span_y
    cells = bricks * pairs * span_z
    owners = min(bricks, rank // 8)
    strip = rank // owners
    count = len(chunk_ends(span_y, slab, groups))
    vmem = lambda *shape: pltpu.VMEM(shape, jnp.float32)
    dma = pltpu.SemaphoreType.DMA
    return pl.pallas_call(
        functools.partial(kernel, (groups, bricks, slab, span_y, span_z, cells)),
        out_shape=(
            jax.ShapeDtypeStruct((slab, span_y, span_z, rank), jnp.float32),
            jax.ShapeDtypeStruct((rank, cols), jnp.float32),
        ),
        in_specs=[pl.BlockSpec(memory_space=pl.ANY), pl.BlockSpec(memory_space=pltpu.VMEM)],
        out_specs=[pl.BlockSpec(memory_space=pltpu.VMEM)] * 2,
        scratch_shapes=[
            vmem(slab + 4, span_y + 2, span_z, cols),
            vmem(slab + 2, span_y + 2, span_z, cols),
            vmem(pairs, span_z, cols),
            vmem(pairs, span_z, rank),
            vmem(pairs, span_z, rank),
            vmem(groups - 1, pairs // groups, span_z, rank),
            vmem(rank, rank),
            vmem(groups * bricks, strip, rank),
            vmem(rank, rank),
            vmem(rank, cols),
            vmem(bricks, strip, cols),
            vmem(rank, cols),
            vmem(rank, 2 * rank),
            dma,
            dma((2, count)),
            dma((2, count)),
            dma((count, groups - 1)),
            dma((count, groups - 1)),
            dma((count, groups - 1)),
            dma((count, groups - 1)),
            dma((2, 2)),
            dma((2, 2)),
        ],
        compiler_params=pltpu.CompilerParams(
            collective_id=0, has_side_effects=True, vmem_limit_bytes=48 * 1024 * 1024
        ),
    )(low_factor, test_matrix)


def solution(mesh):
    return jax.shard_map(
        functools.partial(shards, mesh.shape["grp"], mesh.shape["brick"]),
        mesh=mesh,
        in_specs=(P("brick", None, None, "grp"), P("grp", None)),
        out_specs=(P("brick", None, None, None), P(None, "grp")),
        check_vma=False,
    )
```

time: 380 us -> 109 us (0.29)
  waiting for transfers between devices: 255 us -> 0 us
  Pallas kernels: 0 us -> 103 us
  other arithmetic: 60.1 us -> 0 us
  starting transfers between devices: 20.3 us -> 0 us
  matrix products: 18.1 us -> 0 us
  between operations: 15.3 us -> 0.65 us
  local copies, waits for them, and re-layouts: 10.3 us -> 4.56 us
    psum x3 -> x0, waiting for transfers between devices: 252 us -> none  [the longest x1 89.6 us: shards(): gram = lax.psum(inner_product(sketch, sketch), 'brick')]
    pallas_call x0 -> x1, Pallas kernels: none -> 103 us  [shards(): pl.pallas_call(functools.partial(kernel, (groups, bricks, slab, span_y, s...]
    another operation x9 -> x0, other arithmetic: 53.6 us -> none  [the longest x6 34 us: shards(): lower = jnp.linalg.cholesky(gram)]
    ppermute x4 -> x0, starting transfers between devices: 20 us -> none  [the longest x2 17.4 us: with_halo(): lax.ppermute(lax.slice_in_dim(block, block.shape[dim] - width, None, axis...]
    dot_general x3 -> x0, matrix products: 13.7 us -> none  [the longest x2 10.6 us: inner_product(): lax.dot_general(left, right, (((0,), (0,)), ((), ())), precision=HIGH)]
    another operation x5 -> x0, matrix products: 4.39 us -> none  [the longest x3 3.91 us: shards(): lax.linalg.triangular_solve(lower, sketch, left_side=False, lower=True, t...]
    another operation x9 -> x0, local copies, waits for them, and re-layouts: 3.98 us -> none
    sub x2 -> x0, other arithmetic: 3.88 us -> none  [local_apply(): return inner - DIFF * beside_all - CONV * (xminus - xplus)]
  transfers between devices with their start and end apart: 7 -> 0, of which waited for: 5 -> 0; matrix products, arithmetic and copies ran while one was open for 0% -> 0% of each run, Pallas kernels for 0% -> 0%
where the time goes in v1:
time: 109 us; the launch traced here: 108 us
  Pallas kernels  103 us (94%)
  local copies, waits for them, and re-layouts  4.56 us (4%)
    pallas_call x1, Pallas kernels, shards(): pl.pallas_call(functools.partial(kernel, (groups, bricks, slab, span_y, s...  103 us
    unnamed x6, local copies, waits for them, and re-layouts  4.56 us

profile of v1, /device:TPU:0, one launch (start us, length us, event | category | flops | bytes accessed | tf_op | source)
XLA Modules:
  0.0 108.4 jit_solution(14986207193503955556)
XLA Ops:
  0.6 0.0 copy-start
  0.6 1.6 %copy-done = f32[4,16,32,256]{3,2,1,0:T(8,128)S(1)} copy-done((f32[4,16,32,256]{3,2,1,0:T(8,128)S(1)}, f32[4,16,32,256]{3,2,1,0:T(8,128)}, u32[]{:S(2)}) %copy-start) | copy-done | bytes 2097176
  2.2 0.0 copy-start.1
  2.2 0.9 copy-done.1
  3.2 103.2 %shard_map.41 = (f32[4,16,32,256]{3,2,1,0:T(8,128)S(1)}, f32[256,256]{1,0:T(8,128)S(1)}) custom-call(f32[4,16,32,256]{3,2,1,0:T(8,128)S(1)} %copy-done, f32[256,256]{1,0:T(8,128)S(1)} %copy-done.1), custom_call_target="tpu_custom_call" | custom-call | tf_op jit(solution)/shard_map/pallas_call | solution.py:402
  106.4 1.3 %copy.6 = f32[4,16,32,256]{3,2,1,0:T(8,128)} copy(f32[4,16,32,256]{3,2,1,0:T(8,128)S(1)} %get-tuple-element.4) | data formatting | bytes 4194304
  107.7 0.7 copy.7
Async XLA Ops:
  0.6 1.6 %copy-start = (f32[4,16,32,256]{3,2,1,0:T(8,128)S(1)}, f32[4,16,32,256]{3,2,1,0:T(8,128)}, u32[]{:S(2)}) copy-start(f32[4,16,32,256]{3,2,1,0:T(8,128)} %x_hbm.1) | copy-start | bytes 6291460
  2.2 0.9 copy-start.1

commit v2 on v1

--- a/solution.py
+++ b/solution.py
@@ -12,6 +12,7 @@
 HIGH = lax.Precision.HIGHEST
 MESH = pl.DeviceIdType.MESH
 BLOCK = 32
+GROUP = 8
 
 
 def dot(left, right, dims):
@@ -21,25 +22,23 @@
 
 
 def chunk_ends(span_y, slab_x, groups):
-    count = 4
-    size = span_y // count
-    if span_y % count or size < 3 or (slab_x * size) % groups or (slab_x * 2) % groups:
+    ends = []
+    for end in range(3, span_y, 3):
+        ends.append((end, end - 1, end - 2))
+    ends.append((span_y, span_y, span_y))
+    starts = [0] + [end[2] for end in ends]
+    if any((b - a) * slab_x % groups for a, b in zip(starts, starts[1:])):
         return [(span_y, span_y, span_y)]
-    ends = []
-    for k in range(count):
-        end = size * (k + 1)
-        ends.append((end, end - 1, end - 2) if k < count - 1 else (end, end, end))
     return ends
 
 
 def kernel(
-    dims, x_hbm, omega, basis, projected,
-    ext, first, grown, part, sketch, group_rx, gram, gram_rx, full, proj, proj_rx, proj_full, both,
-    local_sem, halo_send, halo_recv, part_send, part_recv, back_send, back_recv, reduce_sem, gather_sem,
+    dims, x_hbm, omega_hbm, basis, projected,
+    omega, staged, pair_rx, ext, first, grown, part, sketch, group_rx, gram, gram_rx, full, proj, proj_rx, proj_full, both,
+    local_sem, out_sem, pair_sem, halo_send, halo_recv, part_send, part_recv, back_send, back_recv, reduce_sem, gather_sem,
 ):
     groups, bricks, slab, span_y, span_z, cells = dims
-    rank = omega.shape[1]
-    cols = omega.shape[0]
+    cols, rank = omega.shape
     devices = groups * bricks
     me_g = lax.axis_index("grp")
     me_b = lax.axis_index("brick")
@@ -63,9 +62,11 @@
 
     lax.fori_loop(1, devices, greet, 0)
     mine = pltpu.make_async_copy(
-        x_hbm, ext.at[pl.ds(2, slab), pl.ds(1, span_y)], local_sem
+        x_hbm, ext.at[pl.ds(2, slab), pl.ds(1, span_y)], local_sem.at[0]
     )
     mine.start()
+    weights = pltpu.make_async_copy(omega_hbm, omega, local_sem.at[1])
+    weights.start()
     layer = (span_z, cols)
     for y in (0, span_y + 1):
         ext[:, y] = jnp.zeros((slab + 4,) + layer, jnp.float32)
@@ -104,6 +105,7 @@
             halo(k, False).start()
 
     mine.wait()
+    weights.wait()
 
     def operate(mid, low, high, before, after):
         z = lax.broadcasted_iota(jnp.int32, mid.shape, mid.ndim - 2)
@@ -210,14 +212,35 @@
             own_rows(k - 1)
     own_rows(len(ends) - 1)
 
+    half = bricks // 2
+    side = lax.rem(me_b, 2)
+
     def strip_at(o):
-        return pl.ds(pl.multiple_of(o * strip, 8), strip)
-
-    def to_owner(source, sink, sem, d, count, slot):
-        other = lax.rem(me + d, devices) if count == devices else lax.rem(me_b + d, bricks)
-        g = other // bricks if count == devices else me_g
-        o = other - g * bricks if count == devices else other
-        return o, pltpu.make_async_remote_copy(
+        q = lax.rem(o, 2) * (owners // 2) + o // 2
+        return pl.ds(pl.multiple_of(q * strip, 8), strip)
+
+    def half_at(c):
+        return pl.ds(pl.multiple_of(c * (rank // 2), 8), rank // 2)
+
+    pair = pltpu.make_async_remote_copy(
+        src_ref=gram.at[half_at(1 - side)],
+        dst_ref=pair_rx,
+        send_sem=pair_sem.at[0],
+        recv_sem=pair_sem.at[1],
+        device_id=device(me_g, me_b + 1 - 2 * side),
+        device_id_type=MESH,
+    )
+
+    def target(d, paired):
+        if not paired:
+            return me_g, lax.rem(me_b + d, bricks)
+        other = lax.rem(me_g * half + me_b // 2 + d, groups * half)
+        g = other // half
+        return g, (other - g * half) * 2 + side
+
+    def to_owner(source, sink, sem, d, paired, slot):
+        g, o = target(d, paired)
+        return pltpu.make_async_remote_copy(
             src_ref=source.at[strip_at(o)],
             dst_ref=sink.at[slot],
             send_sem=reduce_sem.at[sem, 0],
@@ -232,16 +255,15 @@
         else:
             pl.when(o < owners)(action)
 
-    def scatter_start(source, sink, sem, count, slot):
+    def scatter_start(source, sink, sem, paired, slot):
         def body(d, carry):
             def send():
-                to_owner(source, sink, sem, d, count, slot)[1].start()
-
-            o = lax.rem(me + d, bricks) if count == devices else lax.rem(me_b + d, bricks)
-            guarded(o, send)
+                to_owner(source, sink, sem, d, paired, slot).start()
+
+            guarded(target(d, paired)[1], send)
             return carry
 
-        lax.fori_loop(1, count, body, 0)
+        lax.fori_loop(1, groups * half if paired else bricks, body, 0)
 
         def keep():
             sink[slot] = source[strip_at(me_b)]
@@ -251,7 +273,9 @@
     def bytes_wait(ref, sem):
         pltpu.make_async_copy(ref, ref, sem).wait()
 
-    def scatter_finish(source, sink, sem, count, result):
+    def scatter_finish(source, sink, sem, paired, result):
+        count = groups * half if paired else bricks
+
         def receive():
             bytes_wait(sink.at[pl.ds(0, count - 1)], reduce_sem.at[sem, 1])
 
@@ -261,7 +285,7 @@
             result[strip_at(me_b)] = lax.fori_loop(1, count, add, sink[0])
 
         guarded(me_b, receive)
-        copies = count // bricks * owners
+        copies = groups * owners // 2 if paired else owners
         if owners == bricks:
             bytes_wait(sink.at[pl.ds(0, copies - 1)], reduce_sem.at[sem, 0])
         else:
@@ -306,51 +330,69 @@
             def _():
                 bytes_wait(result.at[...], gather_sem.at[sem, 1])
 
-    scatter_start(gram, gram_rx, 0, devices, me)
+    pair.start()
+
+    def project_piece(k, owner):
+        start, pairs = piece(k)
+        at = pl.ds(start + owner * pairs, pairs)
+        left = sketch[at].reshape(pairs * span_z, rank)
+        right = grown[at].reshape(pairs * span_z, cols)
+        proj[...] += dot(left, right, ((0,), (0,)))
+
+    pair.wait_recv()
+    gram[half_at(side)] += pair_rx[...]
+    scatter_start(gram, gram_rx, 0, True, me_g * half + me_b // 2)
     for k in range(len(ends)):
         for d in range(1, groups):
             back_copy(k, d).start()
-    scatter_finish(gram, gram_rx, 0, devices, full)
+    proj[...] = jnp.zeros_like(proj)
+    for k in range(len(ends)):
+        project_piece(k, me_g)
+    scatter_finish(gram, gram_rx, 0, True, full)
     gather_start(full, 0)
-    gather_finish(full, 0, gram_rx)
+    gather_finish(full, 0, proj_rx)
 
     both[:, 0:rank] = full[...]
     row = lax.broadcasted_iota(jnp.int32, (rank, rank), 0)
     col = lax.broadcasted_iota(jnp.int32, (rank, rank), 1)
     both[:, rank:] = jnp.where(row == col, 1.0, 0.0)
 
-    def project():
-        for k in range(len(ends)):
-            for d in range(1, groups):
-                back_copy(k, d).wait_recv()
-        proj[...] = jnp.zeros_like(proj)
-
-        @pl.loop(0, span_y)
-        def _(y):
-            left = sketch[pl.ds(y * slab, slab)].reshape(slab * span_z, rank)
-            right = grown[pl.ds(y * slab, slab)].reshape(slab * span_z, cols)
-            proj[...] += dot(left, right, ((0,), (0,)))
-
-        scatter_start(proj, proj_rx, 1, bricks, me_b)
+    def project(k):
+        for d in range(1, groups):
+            back_copy(k, d).wait_recv()
+            project_piece(k, lax.rem(me_g + d, groups))
 
     def project_gather():
-        scatter_finish(proj, proj_rx, 1, bricks, proj_full)
+        scatter_finish(proj, proj_rx, 1, False, proj_full)
         gather_start(proj_full, 1)
 
     blocks = rank // BLOCK
+    last = len(ends) - 1
+    hook = blocks // 2 + 1
     for block in range(blocks):
-        if block == blocks // 2:
-            project()
-        if block == blocks - 1:
-            project_gather()
+        if block == hook:
+            for k in range(last + 1):
+                project(k)
+            scatter_start(proj, proj_rx, 1, False, me_b)
         at = block * BLOCK
         panel = both[at : at + BLOCK, :]
-        row = lax.broadcasted_iota(jnp.int32, (BLOCK, 1), 0)
-        for j in range(BLOCK):
-            pivot = panel[j : j + 1, :]
-            scaled = pivot * (1.0 / pivot[:, at + j : at + j + 1])
-            factor = jnp.where(row > j, panel[:, at + j : at + j + 1], 0.0)
-            panel = panel - factor * scaled
+        row = lax.broadcasted_iota(jnp.int32, (BLOCK, 128), 0)
+        for base in range(0, BLOCK, GROUP):
+            columns = [
+                jnp.broadcast_to(panel[:, at + j : at + j + 1], (BLOCK, 128))
+                for j in range(base, base + GROUP)
+            ]
+            for t in range(GROUP):
+                j = base + t
+                over = 1.0 / columns[t][j : j + 1, :]
+                factor = jnp.where(row > j, columns[t], 0.0)
+                for u in range(t + 1, GROUP):
+                    columns[u] = columns[u] - factor * (columns[u][j : j + 1, :] * over)
+                parts = [
+                    panel[:, w : w + 128] - factor * (panel[j : j + 1, w : w + 128] * over)
+                    for w in range(0, 2 * rank, 128)
+                ]
+                panel = jnp.concatenate(parts, axis=1)
         lane = lax.broadcasted_iota(jnp.int32, panel.shape, 1)
         full_row = lax.broadcasted_iota(jnp.int32, panel.shape, 0)
         diagonal = jnp.sum(
@@ -358,10 +400,14 @@
         )
         panel = panel * lax.rsqrt(diagonal)
         both[at : at + BLOCK, :] = panel
-        if block < blocks - 1:
-            below = dot(panel[:, 0:rank], panel, ((0,), (0,)))
-            both[at + BLOCK :, :] = both[at + BLOCK :, :] - below[at + BLOCK :, :]
-
+        done = at + BLOCK
+        if done < rank:
+            floor = done // 128 * 128
+            reach = rank + -(-done // 128) * 128
+            below = dot(panel[:, floor:rank], panel[:, floor:reach], ((0,), (0,)))
+            both[done:, floor:reach] = both[done:, floor:reach] - below[done - floor :, :]
+
+    project_gather()
     inverse = both[:, rank:]
     scaled_inverse = inverse.T * jnp.sqrt(jnp.float32(cells))
     both[:, 0:rank] = scaled_inverse
@@ -370,10 +416,13 @@
     def _(y):
         left = sketch[pl.ds(y * slab, slab)].reshape(slab * span_z, rank)
         value = dot(left, both[:, 0:rank], ((1,), (0,)))
-        basis[:, y] = value.reshape(slab, span_z, rank)
+        staged[:, y] = value.reshape(slab, span_z, rank)
+        pltpu.make_async_copy(staged.at[:, pl.ds(y, 1)], basis.at[:, pl.ds(y, 1)], out_sem).start()
 
     gather_finish(proj_full, 1, proj_rx)
     projected[...] = dot(both[:, rank:], proj_full[...], ((1,), (0,)))
+    pltpu.make_async_copy(staged, basis, out_sem).wait()
+    pair.wait_send()
 
     for k in range(len(ends)):
         @pl.when(me_b < bricks - 1)
@@ -405,9 +454,12 @@
             jax.ShapeDtypeStruct((slab, span_y, span_z, rank), jnp.float32),
             jax.ShapeDtypeStruct((rank, cols), jnp.float32),
         ),
-        in_specs=[pl.BlockSpec(memory_space=pl.ANY), pl.BlockSpec(memory_space=pltpu.VMEM)],
-        out_specs=[pl.BlockSpec(memory_space=pltpu.VMEM)] * 2,
+        in_specs=[pl.BlockSpec(memory_space=pltpu.HBM)] * 2,
+        out_specs=[pl.BlockSpec(memory_space=pltpu.HBM), pl.BlockSpec(memory_space=pltpu.VMEM)],
         scratch_shapes=[
+            vmem(cols, rank),
+            vmem(slab, span_y, span_z, rank),
+            vmem(rank // 2, rank),
             vmem(slab + 4, span_y + 2, span_z, cols),
             vmem(slab + 2, span_y + 2, span_z, cols),
             vmem(pairs, span_z, cols),
@@ -415,13 +467,15 @@
             vmem(pairs, span_z, rank),
             vmem(groups - 1, pairs // groups, span_z, rank),
             vmem(rank, rank),
-            vmem(groups * bricks, strip, rank),
+            vmem(groups * bricks // 2, strip, rank),
             vmem(rank, rank),
             vmem(rank, cols),
             vmem(bricks, strip, cols),
             vmem(rank, cols),
             vmem(rank, 2 * rank),
+            dma((2,)),
             dma,
+            dma((2,)),
             dma((2, count)),
             dma((2, count)),
             dma((count, groups - 1)),

time: 109 us -> 91.1 us (0.84)
  Pallas kernels: 103 us -> 85.7 us
    pallas_call x1, Pallas kernels: 103 us -> 85.7 us  [shards(): pl.pallas_call(functools.partial(kernel, (groups, bricks, slab, span_y, s...]
where the time goes in v2:
time: 91.1 us; the launch traced here: 90.9 us
  Pallas kernels  85.7 us (94%)
  local copies, waits for them, and re-layouts  4.56 us (5%)
    pallas_call x1, Pallas kernels, shards(): pl.pallas_call(functools.partial(kernel, (groups, bricks, slab, span_y, s...  85.7 us
    unnamed x6, local copies, waits for them, and re-layouts  4.56 us

profile of v2, /device:TPU:0, one launch (start us, length us, event | category | flops | bytes accessed | tf_op | source)
XLA Modules:
  0.0 90.9 jit_solution(8358394500394940172)
XLA Ops:
  0.6 0.0 copy-start
  0.6 1.6 %copy-done = f32[4,16,32,256]{3,2,1,0:T(8,128)S(1)} copy-done((f32[4,16,32,256]{3,2,1,0:T(8,128)S(1)}, f32[4,16,32,256]{3,2,1,0:T(8,128)}, u32[]{:S(2)}) %copy-start) | copy-done | bytes 2097176
  2.2 0.0 copy-start.1
  2.2 0.9 %copy-done.1 = f32[256,256]{1,0:T(8,128)S(1)} copy-done((f32[256,256]{1,0:T(8,128)S(1)}, f32[256,256]{1,0:T(8,128)}, u32[]{:S(2)}) %copy-start.1) | copy-done | bytes 262168
  3.2 85.7 %shard_map.41 = (f32[4,16,32,256]{3,2,1,0:T(8,128)S(1)}, f32[256,256]{1,0:T(8,128)S(1)}) custom-call(f32[4,16,32,256]{3,2,1,0:T(8,128)S(1)} %copy-done, f32[256,256]{1,0:T(8,128)S(1)} %copy-done.1), custom_call_target="tpu_custom_call" | custom-call | tf_op jit(solution)/shard_map/pallas_call | solution.py:451
  88.9 1.3 %copy.6 = f32[4,16,32,256]{3,2,1,0:T(8,128)} copy(f32[4,16,32,256]{3,2,1,0:T(8,128)S(1)} %get-tuple-element.4) | data formatting | bytes 4194304
  90.2 0.7 copy.7
Async XLA Ops:
  0.6 1.6 %copy-start = (f32[4,16,32,256]{3,2,1,0:T(8,128)S(1)}, f32[4,16,32,256]{3,2,1,0:T(8,128)}, u32[]{:S(2)}) copy-start(f32[4,16,32,256]{3,2,1,0:T(8,128)} %x_hbm.1) | copy-start | bytes 6291460
  2.2 0.9 %copy-start.1 = (f32[256,256]{1,0:T(8,128)S(1)}, f32[256,256]{1,0:T(8,128)}, u32[]{:S(2)}) copy-start(f32[256,256]{1,0:T(8,128)} %omega_hbm.1) | copy-start | bytes 786436
